TPU v7x, 256 devices: a whole 4x4x8 slice. The times are simulated.
256 devices in a mesh: seq: 16 (over y, x), exp: 16 (over z, core).
Axes of the slice: x: 4, y: 4, z: 8, core: 2. Of those that a mesh axis runs over, the one named last changes fastest.
Arguments:
- x_in: bfloat16 [4096, 8192], P('seq', 'exp'), may hold values from -6 to 6
- z_gate: bfloat16 [4096, 8192], P('seq', 'exp'), may hold values from -6 to 6
- b_in: bfloat16 [4096, 128], P('seq'), may hold values from -0.52734375 to 0.52734375
- c_out: bfloat16 [4096, 128], P('seq'), may hold values from -0.1875 to 0.1875
- dt_step: float32 [4096, 128], P('seq', 'exp'), may hold values from 0.12 to 2052, as said below
- rate: float32 [128], P('exp'), may hold values from 0 to 0.06, as said below
- skip: float32 [128], P('exp'), may hold values from 0.5 to 1.5
- init_state: float32 [128, 64, 128], P('exp'), may hold values from -16.970562 to 16.970562
- residual: bfloat16 [4096, 8192], P(('seq', 'exp')), may hold values from -6 to 6
- norm_gain: float32 [8192], replicated, may hold values from 0.5 to 1.5
- expert_ids: int32 [4096, 2], P(('seq', 'exp')), may hold values from 0 to 15, all different within a row; in each aligned block of 16 rows (0 to 15, 16 to 31, ...) at most 3 rows name the same one
- gate_weights: float32 [4096, 2], P(('seq', 'exp')), may hold values from 0.2 to 1
- w_gate: bfloat16 [16, 8192, 2048], P('exp', None, 'seq'), may hold values from -0.0625 to 0.0625
- w_up: bfloat16 [16, 8192, 2048], P('exp', None, 'seq'), may hold values from -0.0625 to 0.0625
- w_down: bfloat16 [16, 2048, 8192], P('exp', 'seq'), may hold values from -0.125 to 0.125
Outputs:
- layer_out: bfloat16 [4096, 8192], P(('seq', 'exp'))
Inputs may be any that keep to these rules, and one draw needn't show every extreme that they name: `dt_step`: positive step sizes. `rate`: positive rates. `expert_ids`: each row names two different experts; among the rows of one device (aligned blocks of 16 rows) no expert is named by more than 3 rows, and in every draw some expert is named by exactly 3 rows of some block.
All inputs are finite; a program needn't handle non-finite values.
Results may differ from a plain program's by a relative error of at most 0.0095.
Values may be sent and summed in bfloat16 or wider, within the bound.
A program may use at most 128 MiB of HBM per device.

v0:
```python
import jax
import jax.numpy as jnp
from jax import lax
from jax.sharding import PartitionSpec as P

GROUP = 128
PRECISE = lax.Precision.HIGHEST


def entering_2(array, axis, combine, identity):
    devices, mine = (lax.axis_size(axis), lax.axis_index(axis))
    everything = jax.tree.map(
        lambda part, kind: lax.all_gather(part.astype(kind), axis),
        array,
        (jnp.bfloat16, jnp.bfloat16),
    )
    start = jax.tree.map(
        lambda part, zero: jnp.broadcast_to(jnp.asarray(zero, part.dtype), part.shape),
        array,
        identity,
    )

    def hop(k, before):
        reached = k < mine
        new = combine(
            before, jax.tree.map(lambda part, own: part[k].astype(own.dtype), everything, array)
        )
        return jax.tree.map(lambda a, b: jnp.where(reached, a, b), new, before)

    return lax.fori_loop(0, devices, hop, start)


def chain_combine(earlier, later):
    return (earlier[0] + later[0], jnp.exp(later[0])[:, None, None] * earlier[1] + later[1])


def on_device(
    x_in,
    z_gate,
    b_in,
    c_out,
    dt_step,
    rate,
    skip,
    init_state,
    residual,
    norm_gain,
    expert_ids,
    gate_weights,
    w_gate,
    w_up,
    w_down,
):
    token_count, channels = x_in.shape
    heads_here = rate.shape[0]
    head_width = channels // heads_here
    state_width = b_in.shape[1]
    blocks = token_count // GROUP
    inputs = x_in.astype(jnp.float32).reshape(blocks, GROUP, heads_here, head_width)
    keys_in = b_in.astype(jnp.float32).reshape(blocks, GROUP, state_width)
    queries = c_out.astype(jnp.float32).reshape(blocks, GROUP, state_width)
    log_steps = (-rate[None, :] * dt_step).reshape(blocks, GROUP, heads_here)
    cumulative = jnp.cumsum(log_steps, axis=1)
    scores = jnp.einsum("ctn,csn->cts", queries, keys_in, precision=PRECISE)
    causal = jnp.arange(GROUP)[:, None] >= jnp.arange(GROUP)[None, :]
    spread = cumulative[:, :, None, :] - cumulative[:, None, :, :]
    weights = jnp.exp(jnp.where(causal[None, :, :, None], spread, -jnp.inf)) * scores[..., None]
    intra_out = jnp.einsum("ctsh,cshp->cthp", weights, inputs, precision=PRECISE)
    tail_decay = jnp.exp(cumulative[:, -1:, :] - cumulative)
    block_state = jnp.einsum("csh,cshp,csn->chpn", tail_decay, inputs, keys_in, precision=PRECISE)
    block_log = cumulative[:, -1, :]

    def advance(carried, element):
        total_log, total_state = carried
        step_log, step_state = element
        updated = (
            total_log + step_log,
            jnp.exp(step_log)[:, None, None] * total_state + step_state,
        )
        return (updated, (total_log, total_state))

    zero_state = jnp.zeros((heads_here, head_width, state_width), jnp.float32)
    zero_log = jnp.zeros((heads_here,), jnp.float32)
    (device_log, device_state), (enter_log, enter_state) = lax.scan(
        advance, (zero_log, zero_state), (block_log, block_state)
    )
    prior_log, prior_state = entering_2(
        (device_log, device_state), "seq", chain_combine, (zero_log, zero_state)
    )
    incoming = prior_state + jnp.exp(prior_log)[:, None, None] * init_state
    entering = enter_state + jnp.exp(enter_log)[:, :, None, None] * incoming[None]
    inter_out = jnp.exp(cumulative)[..., None] * jnp.einsum(
        "chpn,ctn->cthp", entering, queries, precision=PRECISE
    )
    mixed_out = (intra_out + inter_out + skip[None, None, :, None] * inputs).reshape(
        token_count, channels
    )
    mixer = (mixed_out * jax.nn.silu(z_gate.astype(jnp.float32))).astype(jnp.bfloat16)
    token_mix = lax.all_to_all(mixer, "exp", split_axis=0, concat_axis=1, tiled=True)
    stream = (residual.astype(jnp.float32) + token_mix.astype(jnp.float32)).astype(jnp.bfloat16)
    widened = stream.astype(jnp.float32)
    normed = (
        widened
        * lax.rsqrt(jnp.mean(widened * widened, axis=-1, keepdims=True) + 1e-06)
        * norm_gain[None, :]
    ).astype(jnp.bfloat16)
    rows_here = residual.shape[0]
    owners = lax.axis_size("exp")
    local_experts = w_gate.shape[0]
    experts = owners * local_experts
    capacity = max(2, 2 * rows_here // experts + 1)
    width = residual.shape[1]
    chosen = expert_ids.reshape(-1)
    onehot = (chosen[:, None] == jnp.arange(experts)[None, :]).astype(jnp.int32)
    slot_index = jnp.sum((jnp.cumsum(onehot, axis=0) - onehot) * onehot, axis=1)
    target = chosen * capacity + slot_index
    placing = (target[None, :] == jnp.arange(experts * capacity)[:, None]).astype(jnp.bfloat16)
    pair_rows = jnp.repeat(normed, 2, axis=0)
    outgoing = jnp.dot(placing, pair_rows, preferred_element_type=jnp.float32).astype(jnp.bfloat16)
    outgoing = outgoing.reshape(owners, local_experts, 1, capacity, width)
    arrived = lax.all_to_all(outgoing, "exp", split_axis=0, concat_axis=2, tiled=True)
    segment = lax.all_gather(arrived, "seq", axis=1, tiled=True)
    flattened = segment.reshape(segment.shape[0], -1, segment.shape[-1])
    gate_proj = jnp.einsum("erd,edf->erf", flattened, w_gate, preferred_element_type=jnp.float32)
    up_proj = jnp.einsum("erd,edf->erf", flattened, w_up, preferred_element_type=jnp.float32)
    active = (jax.nn.silu(gate_proj) * up_proj).astype(jnp.bfloat16)
    partial_value = jnp.einsum("erf,efd->erd", active, w_down, preferred_element_type=jnp.float32)
    partials = partial_value.reshape(segment.shape[:-1] + (partial_value.shape[-1],))
    summed = lax.psum_scatter(partials.astype(jnp.bfloat16), "seq", scatter_dimension=1, tiled=True)
    returned = lax.all_to_all(summed, "exp", split_axis=2, concat_axis=0, tiled=True)
    results = returned.reshape(experts * capacity, width)
    picked = results[target].astype(jnp.float32).reshape(rows_here, 2, width)
    mixture = jnp.sum(picked * gate_weights[:, :, None], axis=1)
    return (widened + mixture).astype(jnp.bfloat16)


def solution(mesh):
    return jax.shard_map(
        on_device,
        mesh=mesh,
        in_specs=(
            P("seq", "exp"),
            P("seq", "exp"),
            P("seq", None),
            P("seq", None),
            P("seq", "exp"),
            P("exp"),
            P("exp"),
            P("exp", None, None),
            P(("seq", "exp"), None),
            P(),
            P(("seq", "exp"), None),
            P(("seq", "exp"), None),
            P("exp", None, "seq"),
            P("exp", None, "seq"),
            P("exp", "seq", None),
        ),
        out_specs=P(("seq", "exp"), None),
        check_vma=False,
    )
```

profile of v0, /device:TPU:1, one launch (start us, length us, event | category | flops | bytes accessed | tf_op | source)
XLA Modules:
  0.0 454.0 jit_solution(192723632810441709)
XLA Ops:
  8.6 1.3 reshape.209
  10.6 4.3 while.33
  11.5 1.3 dynamic_update_slice.14
  13.6 1.3 dynamic_update_slice.14
  16.3 1.3 dynamic-slice
  18.5 34.4 %all-reduce = bf16[128]{0:T(256)(128)(2,1)S(1)} all-reduce(bf16[128]{0:T(256)(128)(2,1)S(1)} %dynamic-update-slice), channel_id=2, replica_groups=mesh['seq'=16,'exp'=16] {'seq'}, use_global_device_ids=true, to_apply=%add | all-reduce | flops 128 | bytes 512
  53.7 1.1 copy.84
  55.2 13.5 %all-gather.6.cloned.1.call-done = bf16[128,64,128]{2,1,0:T(8,128)(2,1)} async-done(((bf16[8,64,128]{2,1,0:T(8,128)(2,1)}), bf16[128,64,128]{2,1,0:T(8,128)(2,1)}) %all-gather.6.cloned.1.call-update) | async-done | bytes 2097168 | tf_op jit(solution)/shard_map/all_gather | solution.py:13
  68.7 17.0 %while.34 = (s32[]{:T(128)}, f32[8]{0:T(128)S(1)}, f32[8,64,128]{2,1,0:T(8,128)S(1)}, s32[]{:T(128)}, bf16[16,8]{1,0:T(8,128)(2,1)S(1)}, /*index=5*/bf16[16,8,64,128]{3,2,1,0:T(8,128)(2,1)}, s32[]{:T(128)}, s32[]{:T(128)}) while((s32[]{:T(128)}, f32[8]{0:T(128)S(1)}, f32[8,64,128]{2,1,0:T(8,128)S(1)}, s32[]{:T(128)}, ...), condition=%wide.region_4.5_spmd.clone, body=%wide.region_3.4_spmd.clone.sunk | while | flops 327716 | bytes 655619 | solution.py:30
  85.7 1.0 multiply_add_fusion
  86.7 1.5 fusion.13
  88.2 1.3 fusion.12
  91.0 8.5 %all-to-all-start = ((bf16[16,16,512]{2,1,0:T(8,128)(2,1)}), bf16[16,16,512]{2,1,0:T(8,128)(2,1)S(1)}, u32[]{:S(2)}, u32[]{:S(2)}) async-start(bf16[16,16,512]{2,1,0:T(8,128)(2,1)} %bitcast.12), calls=%async_computation | async-start | bytes 524288 | tf_op jit(solution)/shard_map/all_to_all | solution.py:99
  99.9 11.3 %all-to-all-done = bf16[16,16,512]{2,1,0:T(8,128)(2,1)S(1)} async-done(((bf16[16,16,512]{2,1,0:T(8,128)(2,1)}), bf16[16,16,512]{2,1,0:T(8,128)(2,1)S(1)}, u32[]{:S(2)}, u32[]{:S(2)}) %all-to-all-start) | async-done | bytes 262176 | tf_op jit(solution)/shard_map/all_to_all | solution.py:99
  112.4 1.2 convolution_convert_fusion.1
  113.6 1.5 reshape.174
  115.1 31.2 %all_to_all.34 = bf16[16,1,1,3,8192]{4,3,2,1,0:T(4,128)(2,1)S(1)} all-to-all(bf16[16,1,1,3,8192]{4,3,2,1,0:T(4,128)(2,1)S(1)} %bitcast.114), channel_id=1, replica_groups=mesh['seq'=16,'exp'=16] {'exp'}, dimensions={0} | all-to-all | bytes 1572864 | tf_op jit(solution)/shard_map/all_to_all | solution.py:121
  146.3 1.5 copy.89
  148.0 89.6 %all-gather.8.cloned.1.call-done = bf16[256,1,1,3,8192]{4,0,3,2,1:T(8,128)(2,1)} async-done(((bf16[16,1,1,3,8192]{4,0,3,2,1:T(8,128)(2,1)}), bf16[256,1,1,3,8192]{4,0,3,2,1:T(8,128)(2,1)}) %all-gather.8.cloned.1.call-update) | async-done | bytes 12582928 | tf_op jit(solution)/shard_map/all_gather | solution.py:122
  237.6 18.8 %copy.90 = bf16[256,1,1,3,8192]{4,3,0,2,1:T(4,128)(2,1)} copy(bf16[256,1,1,3,8192]{4,0,3,2,1:T(8,128)(2,1)} %all-gather.8.cloned.1.call-done) | data formatting | bytes 25165824 | tf_op jit(solution)/shard_map/all_gather | solution.py:122
  256.4 26.2 %reshape.175 = bf16[768,8192]{1,0:T(8,128)(2,1)} reshape(bf16[256,1,1,3,8192]{4,3,0,2,1:T(4,128)(2,1)} %copy.90) | data formatting | bytes 25165824 | tf_op jit(solution)/shard_map/reshape.2
  282.7 7.7 %fusion.9 = f32[768,128]{1,0:T(8,128)S(1)} fusion(bf16[768,8192]{1,0:T(8,128)(2,1)} %reshape.175, bf16[1,8192,128]{2,1,0:T(8,128)(2,1)} %param.31), kind=kOutput, calls=%fused_computation.21 | convolution fusion | flops 1610612736 | bytes 15073280 | tf_op jit(solution)/shard_map/erd,edf->erf/dot_general | solution.py:124
  292.0 3.4 fusion.17
  295.6 6.4 %fusion.5 = bf16[1,16,16,3,8192]{4,2,3,1,0:T(8,128)(2,1)} fusion(bf16[1,128,8192]{2,1,0:T(8,128)(2,1)S(1)} %copy-done, bf16[16,16,3,128]{3,2,1,0:T(4,128)(2,1)S(1)} %dot_general.46), kind=kOutput, calls=%fused_computation.16 | convolution fusion | flops 1616904192 | bytes 14876672 | tf_op jit(solution)/shard_map/erf,efd->erd/dot_general | solution.py:127
  302.0 99.5 %reduce-scatter.7.cloned.1.call-done = bf16[1,1,16,3,8192]{4,2,3,1,0:T(8,128)(2,1)} async-done(((bf16[1,16,16,3,8192]{4,2,3,1,0:T(8,128)(2,1)}), bf16[1,1,16,3,8192]{4,2,3,1,0:T(8,128)(2,1)}) %reduce-scatter.7.cloned.1.call-update) | async-done | bytes 786448
  401.5 2.8 copy.92
  404.2 7.9 %all-to-all-start.2 = ((bf16[1,1,16,3,8192]{4,3,1,0,2:T(4,128)(2,1)}), bf16[1,1,16,3,8192]{4,3,1,0,2:T(4,128)(2,1)}, u32[]{:S(2)}, u32[]{:S(2)}) async-start(bf16[1,1,16,3,8192]{4,3,1,0,2:T(4,128)(2,1)} %copy.92), calls=%async_computation.2 | async-start | bytes 2097152 | tf_op jit(solution)/shard_map/all_to_all | solution.py:130
  412.4 27.8 %all-to-all-done.2 = bf16[1,1,16,3,8192]{4,3,1,0,2:T(4,128)(2,1)} async-done(((bf16[1,1,16,3,8192]{4,3,1,0,2:T(4,128)(2,1)}), bf16[1,1,16,3,8192]{4,3,1,0,2:T(4,128)(2,1)}, u32[]{:S(2)}, u32[]{:S(2)}) %all-to-all-start.2) | async-done | bytes 786464 | tf_op jit(solution)/shard_map/all_to_all | solution.py:130
  440.2 1.7 reshape.179
  441.9 1.7 gather_fusion
  443.6 1.7 reshape.183
  445.3 1.4 multiply_reduce_fusion
  (116 shorter events, 29.6 us)
Async XLA Ops:
  6.5 289.0 %copy-start = (bf16[1,128,8192]{2,1,0:T(8,128)(2,1)S(1)}, bf16[1,128,8192]{2,1,0:T(8,128)(2,1)}, u32[]{:S(2)}) copy-start(bf16[1,128,8192]{2,1,0:T(8,128)(2,1)} %param.33) | copy-start | bytes 6291460
  6.5 3.7 copy-start.4
  6.5 62.1 %all-gather.6.cloned.1.call-start = ((), (), s32[]{:S(2)}) async-start(), calls=%async_computation.4 | async-start | bytes 2228224 | tf_op jit(solution)/shard_map/all_gather | solution.py:13
  10.6 44.2 %copy-start.7 = (s32[16,2]{0,1:T(2,128)S(1)}, s32[16,2]{0,1:T(2,128)}, u32[]{:S(2)}) copy-start(s32[16,2]{0,1:T(2,128)} %param.29) | copy-start | bytes 388
  10.6 44.4 %copy-start.2 = (bf16[256,128]{1,0:T(8,128)(2,1)S(1)}, bf16[256,128]{1,0:T(8,128)(2,1)}, u32[]{:S(2)}) copy-start(bf16[256,128]{1,0:T(8,128)(2,1)} %param.22) | copy-start | bytes 196612
  68.7 19.5 %copy-start.6 = (f32[2,128,8]{1,2,0:T(8,128)S(1)}, f32[2,128,8]{1,2,0:T(8,128)}, u32[]{:S(2)}) copy-start(f32[2,128,8]{1,2,0:T(8,128)} %copy.76) | copy-start | bytes 24580
  68.7 19.5 %copy-start.10 = (f32[8]{0:T(128)S(1)}, f32[8]{0:T(128)}, u32[]{:S(2)}) copy-start(f32[8]{0:T(128)} %param.25) | copy-start | bytes 100
  90.0 21.4 %copy-start.3 = (bf16[16,8192]{1,0:T(8,128)(2,1)S(1)}, bf16[16,8192]{1,0:T(8,128)(2,1)}, u32[]{:S(2)}) copy-start(bf16[16,8192]{1,0:T(8,128)(2,1)} %param.27) | copy-start | bytes 786436
  90.2 21.4 %copy-start.5 = (f32[8192]{0:T(1024)S(1)}, f32[8192]{0:T(1024)}, u32[]{:S(2)}) copy-start(f32[8192]{0:T(1024)} %param.28) | copy-start | bytes 98308
  91.0 20.2 %all-to-all-start = ((bf16[16,16,512]{2,1,0:T(8,128)(2,1)}), bf16[16,16,512]{2,1,0:T(8,128)(2,1)S(1)}, u32[]{:S(2)}, u32[]{:S(2)}) async-start(bf16[16,16,512]{2,1,0:T(8,128)(2,1)} %bitcast.12), calls=%async_computation | async-start | bytes 524288 | tf_op jit(solution)/shard_map/all_to_all | solution.py:99
  99.6 138.0 %all-gather.8.cloned.1.call-start = ((), (), s32[]{:S(2)}) async-start(), calls=%async_computation.5 | async-start | bytes 13369344 | tf_op jit(solution)/shard_map/all_gather | solution.py:122
  147.8 253.7 %reduce-scatter.7.cloned.1.call-start = ((), (), s32[]{:S(2)}) async-start(), calls=%async_computation.6 | async-start | bytes 13369344
  282.7 8.8 %copy-start.1 = (bf16[768,8192]{1,0:T(8,128)(2,1)S(1)}, bf16[768,8192]{1,0:T(8,128)(2,1)}, u32[]{:S(2)}) copy-start(bf16[768,8192]{1,0:T(8,128)(2,1)} %reshape.175) | copy-start | bytes 37748740
  282.7 9.4 %copy-start.9 = (bf16[1,8192,128]{2,1,0:T(8,128)(2,1)S(1)}, bf16[1,8192,128]{2,1,0:T(8,128)(2,1)}, u32[]{:S(2)}) copy-start(bf16[1,8192,128]{2,1,0:T(8,128)(2,1)} %param.32) | copy-start | bytes 6291460
  302.0 110.4 %copy-start.8 = (f32[16,2]{0,1:T(2,128)S(1)}, f32[16,2]{0,1:T(2,128)}, u32[]{:S(2)}) copy-start(f32[16,2]{0,1:T(2,128)} %param.30) | copy-start | bytes 388
  404.2 35.9 %all-to-all-start.2 = ((bf16[1,1,16,3,8192]{4,3,1,0,2:T(4,128)(2,1)}), bf16[1,1,16,3,8192]{4,3,1,0,2:T(4,128)(2,1)}, u32[]{:S(2)}, u32[]{:S(2)}) async-start(bf16[1,1,16,3,8192]{4,3,1,0,2:T(4,128)(2,1)} %copy.92), calls=%async_computation.2 | async-start | bytes 2097152 | tf_op jit(solution)/shard_map/all_to_all | solution.py:130
Sparse Core Ops, SparseCore 0:
  15.7 52.9 all-gather.5
  147.9 89.6 all-gather.7
  302.1 99.3 reduce-scatter.6
where the time goes:
time: 456 us; the launch traced here: 454 us
  waiting for transfers between devices  242 us (53%)
  local copies, waits for them, and re-layouts  68.5 us (15%)
  blocking collectives  65.6 us (14%)
  other arithmetic  24.9 us (5%)
  matrix products  22.1 us (5%)
  starting transfers between devices  16.7 us (4%)
  between operations  14.1 us (3%)
    unnamed x4, waiting for transfers between devices  99.5 us
    all_gather x1, waiting for transfers between devices, on_device(): segment = lax.all_gather(arrived, 'seq', axis=1, tiled=True)  89.6 us
    unnamed x1, blocking collectives  34.4 us
    all_to_all x1, blocking collectives, on_device(): lax.all_to_all(outgoing, 'exp', split_axis=0, concat_axis=2, tiled=True)  31.2 us
    all_to_all x1, waiting for transfers between devices, on_device(): lax.all_to_all(summed, 'exp', split_axis=2, concat_axis=0, tiled=True)  27.8 us
    another operation x1, local copies, waits for them, and re-layouts  26.2 us
    all_gather x1, local copies, waits for them, and re-layouts, on_device(): segment = lax.all_gather(arrived, 'seq', axis=1, tiled=True)  18.8 us
    select_n x16, other arithmetic, hop(): return jax.tree.map(lambda a, b: jnp.where(reached, a, b), new, before)  16.2 us
  transfers between devices with their start and end apart: 5, of which 5 were waited for; matrix products, arithmetic and copies ran while one was open for 1% of the time, Pallas kernels for 0%

commit v1 on v0

--- a/solution.py
+++ b/solution.py
@@ -2,6 +2,7 @@
 import jax.numpy as jnp
 from jax import lax
 from jax.sharding import PartitionSpec as P
+from jax.lax import all_to_all, axis_size
 
 GROUP = 128
 PRECISE = lax.Precision.HIGHEST
@@ -51,6 +52,13 @@
     w_up,
     w_down,
 ):
+
+    def define_works_on(page, dim_i):
+        plain = axis_size("seq")
+        answer = jnp.stack([page] * plain)
+        block_last = all_to_all(answer, "seq", 0, 0)
+        return jnp.concatenate(block_last, dim_i)
+
     token_count, channels = x_in.shape
     heads_here = rate.shape[0]
     head_width = channels // heads_here
@@ -119,7 +127,7 @@
     outgoing = jnp.dot(placing, pair_rows, preferred_element_type=jnp.float32).astype(jnp.bfloat16)
     outgoing = outgoing.reshape(owners, local_experts, 1, capacity, width)
     arrived = lax.all_to_all(outgoing, "exp", split_axis=0, concat_axis=2, tiled=True)
-    segment = lax.all_gather(arrived, "seq", axis=1, tiled=True)
+    segment = define_works_on(arrived, 1)
     flattened = segment.reshape(segment.shape[0], -1, segment.shape[-1])
     gate_proj = jnp.einsum("erd,edf->erf", flattened, w_gate, preferred_element_type=jnp.float32)
     up_proj = jnp.einsum("erd,edf->erf", flattened, w_up, preferred_element_type=jnp.float32)

time: 456 us -> 504 us (1.11)
  blocking collectives: 65.6 us -> 212 us
  waiting for transfers between devices: 242 us -> 145 us
    all_to_all x0 -> x1, blocking collectives: none -> 146 us  [define_works_on(): block_last = all_to_all(answer, 'seq', 0, 0)]
    all_gather x1 -> x0, waiting for transfers between devices: 89.6 us -> none  [on_device(): segment = lax.all_gather(arrived, 'seq', axis=1, tiled=True)]
    all_gather x1 -> x0, local copies, waits for them, and re-layouts: 18.8 us -> none  [on_device(): segment = lax.all_gather(arrived, 'seq', axis=1, tiled=True)]
    all_to_all x1, local copies, waits for them, and re-layouts: 1.46 us -> 12.1 us  [define_works_on(): block_last = all_to_all(answer, 'seq', 0, 0)]
    unnamed x4 -> x3, waiting for transfers between devices: 99.5 us -> 92.2 us
    another operation x1 -> x3, local copies, waits for them, and re-layouts: 26.2 us -> 33 us
  transfers between devices with their start and end apart: 5 -> 4, of which waited for: 5 -> 4; matrix products, arithmetic and copies ran while one was open for 1% -> 1% of each run, Pallas kernels for 0% -> 0%
where the time goes in v1:
time: 504 us; the launch traced here: 502 us
  blocking collectives  212 us (42%)
  waiting for transfers between devices  145 us (29%)
  local copies, waits for them, and re-layouts  67 us (13%)
  other arithmetic  24.9 us (5%)
  matrix products  22 us (4%)
  starting transfers between devices  16.5 us (3%)
  between operations  14.4 us (3%)
    all_to_all x1, blocking collectives, define_works_on(): block_last = all_to_all(answer, 'seq', 0, 0)  146 us
    unnamed x3, waiting for transfers between devices  92.2 us
    unnamed x1, blocking collectives  34.3 us
    all_to_all x1, blocking collectives, on_device(): lax.all_to_all(outgoing, 'exp', split_axis=0, concat_axis=2, tiled=True)  31.2 us
    all_to_all x1, waiting for transfers between devices, on_device(): lax.all_to_all(summed, 'exp', split_axis=2, concat_axis=0, tiled=True)  27.8 us
    another operation x1, local copies, waits for them, and re-layouts  26.3 us
    select_n x16, other arithmetic, hop(): return jax.tree.map(lambda a, b: jnp.where(reached, a, b), new, before)  16.2 us
    all_gather x1, waiting for transfers between devices, entering_2(): lax.all_gather(part.astype(kind), axis)  13.6 us
  transfers between devices with their start and end apart: 4, of which 4 were waited for; matrix products, arithmetic and copies ran while one was open for 1% of the time, Pallas kernels for 0%

profile of v1, /device:TPU:1, one launch (start us, length us, event | category | flops | bytes accessed | tf_op | source)
XLA Modules:
  0.0 501.9 jit_solution(8072472494756127829)
XLA Ops:
  8.6 1.3 reshape.211
  10.6 4.2 while.33
  11.5 1.3 dynamic_update_slice.14
  13.6 1.3 dynamic_update_slice.14
  16.3 1.3 dynamic-slice
  18.4 34.3 %all-reduce = bf16[128]{0:T(256)(128)(2,1)S(1)} all-reduce(bf16[128]{0:T(256)(128)(2,1)S(1)} %dynamic-update-slice), channel_id=2, replica_groups=mesh['seq'=16,'exp'=16] {'seq'}, use_global_device_ids=true, to_apply=%add | all-reduce | flops 128 | bytes 512
  53.5 1.1 copy.84
  55.0 13.6 %all-gather.4.cloned.1.call-done = bf16[128,64,128]{2,1,0:T(8,128)(2,1)} async-done(((bf16[8,64,128]{2,1,0:T(8,128)(2,1)}), bf16[128,64,128]{2,1,0:T(8,128)(2,1)}) %all-gather.4.cloned.1.call-update) | async-done | bytes 2097168 | tf_op jit(solution)/shard_map/all_gather | solution.py:14
  68.7 17.0 %while.34 = (s32[]{:T(128)}, f32[8]{0:T(128)S(1)}, f32[8,64,128]{2,1,0:T(8,128)S(1)}, s32[]{:T(128)}, bf16[16,8]{1,0:T(8,128)(2,1)S(1)}, /*index=5*/bf16[16,8,64,128]{3,2,1,0:T(8,128)(2,1)}, s32[]{:T(128)}, s32[]{:T(128)}) while((s32[]{:T(128)}, f32[8]{0:T(128)S(1)}, f32[8,64,128]{2,1,0:T(8,128)S(1)}, s32[]{:T(128)}, ...), condition=%wide.region_4.5_spmd.clone, body=%wide.region_3.4_spmd.clone.sunk | while | flops 327716 | bytes 655619 | solution.py:31
  86.7 1.5 fusion.13
  88.2 1.3 fusion.12
  91.0 8.5 %all-to-all-start = ((bf16[16,16,512]{2,1,0:T(8,128)(2,1)}), bf16[16,16,512]{2,1,0:T(8,128)(2,1)S(1)}, u32[]{:S(2)}, u32[]{:S(2)}) async-start(bf16[16,16,512]{2,1,0:T(8,128)(2,1)} %bitcast.12), calls=%async_computation | async-start | bytes 524288 | tf_op jit(solution)/shard_map/all_to_all | solution.py:107
  99.9 11.3 %all-to-all-done = bf16[16,16,512]{2,1,0:T(8,128)(2,1)S(1)} async-done(((bf16[16,16,512]{2,1,0:T(8,128)(2,1)}), bf16[16,16,512]{2,1,0:T(8,128)(2,1)S(1)}, u32[]{:S(2)}, u32[]{:S(2)}) %all-to-all-start) | async-done | bytes 262176 | tf_op jit(solution)/shard_map/all_to_all | solution.py:107
  112.3 1.2 convolution_convert_fusion.1
  113.6 1.5 reshape.178
  115.0 31.2 %all_to_all.36 = bf16[16,1,1,3,8192]{4,3,2,1,0:T(4,128)(2,1)S(1)} all-to-all(bf16[16,1,1,3,8192]{4,3,2,1,0:T(4,128)(2,1)S(1)} %bitcast.115), channel_id=1, replica_groups=mesh['seq'=16,'exp'=16] {'exp'}, dimensions={0} | all-to-all | bytes 1572864 | tf_op jit(solution)/shard_map/all_to_all | solution.py:129
  146.9 6.1 %stack.5 = bf16[16,1,1,16,3,8192]{5,3,4,2,1,0:T(8,128)(2,1)} broadcast(bf16[16,3,8192]{2,0,1:T(8,128)(2,1)S(1)} %copy.89), dimensions={3,4,5} | broadcast | bytes 13369344 | tf_op jit(solution)/shard_map/stack | solution.py:58
  153.0 146.2 %all_to_all.37 = bf16[16,1,1,16,3,8192]{5,3,4,2,1,0:T(8,128)(2,1)S(1)} all-to-all(bf16[16,1,1,16,3,8192]{5,3,4,2,1,0:T(8,128)(2,1)} %stack.5), channel_id=1, replica_groups=mesh['seq'=16,'exp'=16] {'seq'}, dimensions={0} | all-to-all | bytes 25165824 | tf_op jit(solution)/shard_map/all_to_all | solution.py:59
  299.2 12.1 %copy.90 = bf16[16,1,1,16,3,8192]{5,4,3,0,2,1:T(4,128)(2,1)} copy(bf16[16,1,1,16,3,8192]{5,3,4,2,1,0:T(8,128)(2,1)S(1)} %all_to_all.37) | data formatting | bytes 25165824 | tf_op jit(solution)/shard_map/all_to_all | solution.py:59
  311.3 26.3 %reshape.179 = bf16[768,8192]{1,0:T(8,128)(2,1)} reshape(bf16[16,1,1,16,3,8192]{5,4,3,0,2,1:T(4,128)(2,1)} %copy.90) | data formatting | bytes 25165824 | tf_op jit(solution)/shard_map/reshape.4
  337.6 7.7 %fusion.9 = f32[768,128]{1,0:T(8,128)S(1)} fusion(bf16[768,8192]{1,0:T(8,128)(2,1)} %reshape.179, bf16[1,8192,128]{2,1,0:T(8,128)(2,1)} %param.31), kind=kOutput, calls=%fused_computation.21 | convolution fusion | flops 1610612736 | bytes 15073280 | tf_op jit(solution)/shard_map/erd,edf->erf/dot_general | solution.py:132
  345.3 1.1 copy-done.1
  347.0 3.4 fusion.17
  350.5 6.3 %fusion.5 = bf16[1,16,16,3,8192]{4,2,3,1,0:T(8,128)(2,1)} fusion(bf16[1,128,8192]{2,1,0:T(8,128)(2,1)S(1)} %copy-done, bf16[16,16,3,128]{3,2,1,0:T(4,128)(2,1)S(1)} %dot_general.46), kind=kOutput, calls=%fused_computation.16 | convolution fusion | flops 1616904192 | bytes 14876672 | tf_op jit(solution)/shard_map/erf,efd->erd/dot_general | solution.py:135
  356.9 92.1 %reduce-scatter.7.cloned.1.call-done = bf16[1,1,16,3,8192]{4,2,3,1,0:T(8,128)(2,1)} async-done(((bf16[1,16,16,3,8192]{4,2,3,1,0:T(8,128)(2,1)}), bf16[1,1,16,3,8192]{4,2,3,1,0:T(8,128)(2,1)}) %reduce-scatter.7.cloned.1.call-update) | async-done | bytes 786448
  449.0 2.8 copy.92
  451.8 7.9 %all-to-all-start.3 = ((bf16[1,1,16,3,8192]{4,3,1,0,2:T(4,128)(2,1)}), bf16[1,1,16,3,8192]{4,3,1,0,2:T(4,128)(2,1)}, u32[]{:S(2)}, u32[]{:S(2)}) async-start(bf16[1,1,16,3,8192]{4,3,1,0,2:T(4,128)(2,1)} %copy.92), calls=%async_computation.3 | async-start | bytes 2097152 | tf_op jit(solution)/shard_map/all_to_all | solution.py:138
  460.0 27.8 %all-to-all-done.3 = bf16[1,1,16,3,8192]{4,3,1,0,2:T(4,128)(2,1)} async-done(((bf16[1,1,16,3,8192]{4,3,1,0,2:T(4,128)(2,1)}), bf16[1,1,16,3,8192]{4,3,1,0,2:T(4,128)(2,1)}, u32[]{:S(2)}, u32[]{:S(2)}) %all-to-all-start.3) | async-done | bytes 786464 | tf_op jit(solution)/shard_map/all_to_all | solution.py:138
  487.7 1.7 reshape.183
  489.5 1.7 gather_fusion
  491.1 1.7 reshape.187
  492.8 1.4 multiply_reduce_fusion
  (115 shorter events, 30.0 us)
Async XLA Ops:
  6.5 344.0 %copy-start = (bf16[1,128,8192]{2,1,0:T(8,128)(2,1)S(1)}, bf16[1,128,8192]{2,1,0:T(8,128)(2,1)}, u32[]{:S(2)}) copy-start(bf16[1,128,8192]{2,1,0:T(8,128)(2,1)} %param.33) | copy-start | bytes 6291460
  6.5 3.7 copy-start.4
  6.5 62.1 %all-gather.4.cloned.1.call-start = ((), (), s32[]{:S(2)}) async-start(), calls=%async_computation.5 | async-start | bytes 2228224 | tf_op jit(solution)/shard_map/all_gather | solution.py:14
  10.6 44.0 %copy-start.7 = (s32[16,2]{0,1:T(2,128)S(1)}, s32[16,2]{0,1:T(2,128)}, u32[]{:S(2)}) copy-start(s32[16,2]{0,1:T(2,128)} %param.29) | copy-start | bytes 388
  10.6 44.2 %copy-start.2 = (bf16[256,128]{1,0:T(8,128)(2,1)S(1)}, bf16[256,128]{1,0:T(8,128)(2,1)}, u32[]{:S(2)}) copy-start(bf16[256,128]{1,0:T(8,128)(2,1)} %param.22) | copy-start | bytes 196612
  68.7 19.5 %copy-start.6 = (f32[2,128,8]{1,2,0:T(8,128)S(1)}, f32[2,128,8]{1,2,0:T(8,128)}, u32[]{:S(2)}) copy-start(f32[2,128,8]{1,2,0:T(8,128)} %copy.76) | copy-start | bytes 24580
  68.7 19.5 %copy-start.10 = (f32[8]{0:T(128)S(1)}, f32[8]{0:T(128)}, u32[]{:S(2)}) copy-start(f32[8]{0:T(128)} %param.25) | copy-start | bytes 100
  90.0 21.4 %copy-start.3 = (bf16[16,8192]{1,0:T(8,128)(2,1)S(1)}, bf16[16,8192]{1,0:T(8,128)(2,1)}, u32[]{:S(2)}) copy-start(bf16[16,8192]{1,0:T(8,128)(2,1)} %param.27) | copy-start | bytes 786436
  90.1 21.4 %copy-start.5 = (f32[8192]{0:T(1024)S(1)}, f32[8192]{0:T(1024)}, u32[]{:S(2)}) copy-start(f32[8192]{0:T(1024)} %param.28) | copy-start | bytes 98308
  91.0 20.2 %all-to-all-start = ((bf16[16,16,512]{2,1,0:T(8,128)(2,1)}), bf16[16,16,512]{2,1,0:T(8,128)(2,1)S(1)}, u32[]{:S(2)}, u32[]{:S(2)}) async-start(bf16[16,16,512]{2,1,0:T(8,128)(2,1)} %bitcast.12), calls=%async_computation | async-start | bytes 524288 | tf_op jit(solution)/shard_map/all_to_all | solution.py:107
  99.5 349.5 %reduce-scatter.7.cloned.1.call-start = ((), (), s32[]{:S(2)}) async-start(), calls=%async_computation.6 | async-start | bytes 13369344
  337.6 8.8 %copy-start.1 = (bf16[768,8192]{1,0:T(8,128)(2,1)S(1)}, bf16[768,8192]{1,0:T(8,128)(2,1)}, u32[]{:S(2)}) copy-start(bf16[768,8192]{1,0:T(8,128)(2,1)} %reshape.179) | copy-start | bytes 37748740
  337.6 9.4 %copy-start.9 = (bf16[1,8192,128]{2,1,0:T(8,128)(2,1)S(1)}, bf16[1,8192,128]{2,1,0:T(8,128)(2,1)}, u32[]{:S(2)}) copy-start(bf16[1,8192,128]{2,1,0:T(8,128)(2,1)} %param.32) | copy-start | bytes 6291460
  356.9 103.0 %copy-start.8 = (f32[16,2]{0,1:T(2,128)S(1)}, f32[16,2]{0,1:T(2,128)}, u32[]{:S(2)}) copy-start(f32[16,2]{0,1:T(2,128)} %param.30) | copy-start | bytes 388
  451.8 35.9 %all-to-all-start.3 = ((bf16[1,1,16,3,8192]{4,3,1,0,2:T(4,128)(2,1)}), bf16[1,1,16,3,8192]{4,3,1,0,2:T(4,128)(2,1)}, u32[]{:S(2)}, u32[]{:S(2)}) async-start(bf16[1,1,16,3,8192]{4,3,1,0,2:T(4,128)(2,1)} %copy.92), calls=%async_computation.3 | async-start | bytes 2097152 | tf_op jit(solution)/shard_map/all_to_all | solution.py:138
Sparse Core Ops, SparseCore 0:
  15.7 52.9 all-gather.3
  357.0 91.9 reduce-scatter.6
